TPU v7x, 32 devices: a whole 2x2x4 slice. The times are simulated.
32 devices in a mesh: user: 8 (over y, x, core), item: 4 (over z).
Axes of the slice: x: 2, y: 2, z: 4, core: 2. Of those that a mesh axis runs over, the one named last changes fastest.
Arguments:
- user_factors: float32 [4096, 256], P('user'), may hold values from -1.5 to 1.5
- item_factors: float32 [32768, 256], P(('user', 'item')), may hold values from -1.5 to 1.5
- feedback: bfloat16 [128, 4096, 128], P('item', 'user'), may hold values from 0 to 1
- item_pick: int32 [32, 32], replicated, may hold values from 0 to 7, as said below
- user_noise: float32 [4096, 256], P('user'), may hold values from -6 to 6
- item_noise: float32 [32768, 256], P(('user', 'item')), may hold values from -6 to 6
Outputs:
- new_user: float32 [4096, 256], P('user')
- new_item: float32 [32768, 256], P(('user', 'item'))
Inputs may be any that keep to these rules, and one draw needn't show every extreme that they name: For every owner o and every user slab u, the 4 entries item_pick[u * 4 + i, o] are distinct, so that no tile appears twice.
All inputs are finite; a program needn't handle non-finite values.
Results may differ from a plain program's by a relative error of at most 0.00058.
Values may be sent and summed in bfloat16 or wider, within the bound.
A program may use at most 192 MiB of HBM per device.

v0:
```python
import functools
import math

import jax
import jax.numpy as jnp
from jax import lax
from jax.experimental import pallas as pl
from jax.experimental.pallas import tpu as pltpu
from jax.sharding import PartitionSpec as P

step_size = 0.01
item_step = 0.1
prior_weight = 1.0
noise_scale = math.sqrt(0.02)
item_noise_scale = math.sqrt(0.2)

FACTOR_BOUND = 1.5
LEVELS = 32766.0
RUN = 2
PAD = 8


def encode(ref, value, unit):
    rows = value.shape[0]
    largest = jnp.max(jnp.abs(value), axis=0, keepdims=True)
    count = jnp.floor(largest * (1.0 / (LEVELS * unit))) + 1.0
    inverse = 1.0 / (count * unit)
    ref[pl.ds(0, rows), :] = jnp.round(value * inverse).astype(jnp.int32).astype(jnp.int16)
    ref[pl.ds(rows, PAD), :] = jnp.broadcast_to(count, (PAD, value.shape[1])).astype(jnp.int32).astype(jnp.int16)


def decode(ref, weight):
    rows = ref.shape[0] - PAD
    count = ref[pl.ds(rows, PAD), :].astype(jnp.float32)[0:1]
    return ref[pl.ds(0, rows), :].astype(jnp.float32) * (count * weight)


def kernel(
    U, Z, pick, items_wide, user_wide, feedback, item_out, user_out, *scratch
):
    zbufs = scratch[: 2 * (Z - 1)]
    (items, user, og, arr, gs, gr, cs, cr, crd, fb, us, ur, ugs, ugr, ug, zsend, zrecv, isend, irecv, gsend, grecv,
     csend, crecv, cdrecv, fsem, usend, urecv, vsend, vrecv) = scratch[2 * (Z - 1):]
    B, T, K = items.shape
    N = user.shape[0]
    piece = N // Z
    me = lax.axis_index("user")
    z = lax.axis_index("item")
    item_unit = N * FACTOR_BOUND * U / LEVELS / 32000.0
    user_unit = U * Z * T * FACTOR_BOUND * Z / LEVELS / 32000.0

    def far(axis, to, src, dst, ssem, rsem):
        return pltpu.make_async_remote_copy(
            src_ref=src, dst_ref=dst, send_sem=ssem, recv_sem=rsem,
            device_id={axis: to}, device_id_type=pl.DeviceIdType.MESH)

    barrier = pltpu.get_barrier_semaphore()

    items[...] = items_wide[...].astype(jnp.bfloat16)

    def greet_user(j, c):
        pl.semaphore_signal(barrier, inc=1, device_id={"user": lax.rem(me + j, U)}, device_id_type=pl.DeviceIdType.MESH)
        return c

    lax.fori_loop(1, U, greet_user, 0)
    for j in range(1, Z):
        pl.semaphore_signal(barrier, inc=1, device_id={"item": lax.rem(z + j, Z)}, device_id_type=pl.DeviceIdType.MESH)
    pl.semaphore_wait(barrier, U - 1 + Z - 1)

    def zcopy(d, way):
        src = items if d == 1 else zbufs[2 * (d - 2) + way]
        k = 2 * (d - 1) + way
        return far("item", z + (1 if way == 0 else -1), src, zbufs[k], zsend.at[k], zrecv.at[k])

    def can_send(d, way):
        return (z - (d - 1) >= 0) & (z + 1 < Z) if way == 0 else (z + (d - 1) < Z) & (z >= 1)

    def comes(d, way):
        return z - d >= 0 if way == 0 else z + d < Z

    for way in (0, 1):
        pl.when(can_send(1, way))(lambda way=way: zcopy(1, way).start())

    user[...] = user_wide[...].astype(jnp.bfloat16)
    ug[...] = jnp.zeros_like(ug)

    def icopy(p, to, src):
        return far("user", to, og.at[p, to], arr.at[p, src], isend.at[p, to], irecv.at[p, src])

    def spread(p, blocks):
        def one(j, c):
            to = lax.rem(me + j, U)
            og[p, to] = blocks[pick[to * Z + z, me * Z + p]]
            icopy(p, to, me).start()
            return c
        lax.fori_loop(1, U, one, 0)
        arr[p, me] = blocks[pick[me * Z + z, me * Z + p]]

    def gcopy(p, to, src):
        return far("user", to, gs.at[p, to], gr.at[p, src], gsend.at[p, to], grecv.at[p, src])

    def fcopy(p, pair, slot):
        return pltpu.make_async_copy(feedback.at[pl.ds(2 * pair, 2), p], fb.at[slot], fsem.at[slot])

    pairs = U // 2

    def pair_of(j):
        return lax.rem(me // 2 + pairs - j, pairs)

    def compute(p):
        fcopy(p, pair_of(0), 0).start()

        def one(j, c):
            pair = pair_of(j)
            slot = lax.rem(j, 2)

            @pl.when(j + 1 < pairs)
            def _():
                fcopy(p, pair_of(j + 1), 1 - slot).start()

            for t in range(2):
                o = 2 * pair + t
                pl.when(o != me)(lambda o=o: icopy(p, me, o).wait_recv())
            fcopy(p, pair, slot).wait()
            tile = arr[p, pl.ds(2 * pair, 2)].reshape(2 * T, K)
            scores = lax.dot_general(user[...], tile, (((1,), (1,)), ((), ())), preferred_element_type=jnp.float32)
            target = jnp.concatenate([fb[slot, 0], fb[slot, 1]], axis=1).astype(jnp.float32)
            residual = (0.5 * jnp.tanh(0.5 * scores) + (0.5 - target)).astype(jnp.bfloat16)
            part = lax.dot_general(residual, user[...], (((0,), (0,)), ((), ())), preferred_element_type=jnp.float32)
            for t in range(2):
                o = 2 * pair + t
                value = part[t * T:(t + 1) * T]

                @pl.when(o != me)
                def _():
                    encode(gs.at[p, o], value, item_unit)
                    gcopy(p, o, me).start()

                @pl.when(o == me)
                def _():
                    encode(gr.at[p, me], value, item_unit)
            ug[...] += jnp.dot(residual, tile, preferred_element_type=jnp.float32)
            return c

        lax.fori_loop(0, pairs, one, 0)

    def dense(p, b):
        def one(u, acc):
            weight = jnp.where(pick[u * Z + z, me * Z + p] == b, item_unit, 0.0).astype(jnp.float32)
            return acc + decode(gr.at[p, u], weight)
        return lax.fori_loop(0, U, one, jnp.zeros((T, K), jnp.float32))

    def await_grads(p):
        def one(j, c):
            gcopy(p, me, lax.rem(me + j, U)).wait_recv()
            return c
        lax.fori_loop(1, U, one, 0)

    def run(b):
        return pl.ds(b * RUN, RUN)

    def up_copy(to, p, c):
        return far("item", to, cs.at[p, run(c)], cr.at[p, run(c)], csend.at[p, c], crecv.at[p, c])

    def last_copy(to, p, c):
        return far("item", to, cs.at[p, run(c)], crd.at[run(c)], csend.at[p, c], cdrecv.at[c])

    def pass_on(p, c, way, relay):
        to = z + (1 if way == 0 else -1)
        if relay:
            up_copy(z, p, c).wait_recv()

        def one(i, carry):
            b = c * RUN + i
            total = dense(p, b)
            if relay:
                total = total + decode(cr.at[p, b], item_unit)
            encode(cs.at[p, b], total, item_unit)
            return carry
        lax.fori_loop(0, RUN, one, 0)
        if way == 0:
            up_copy(to, p, c).start()
        else:
            pl.when(to == p)(lambda: last_copy(to, p, c).start())
            pl.when(to != p)(lambda: up_copy(to, p, c).start())

    def chain(p, way):
        await_grads(p)

        def one(c, carry):
            pass_on(p, c, way, False)
            return carry
        lax.fori_loop(0, B // RUN, one, 0)

    def plane(d, way):
        return z - d if way == 0 else z + d

    def start_chain(d, way):
        out = 1 - way
        edge = z == 0 if out == 0 else z == Z - 1

        @pl.when(comes(d, way) & edge)
        def _():
            chain(plane(d, way), out)

    spread(z, items)
    compute(z)
    for d in range(1, Z):
        for way in (0, 1):
            @pl.when(comes(d, way))
            def _(d=d, way=way):
                zcopy(d, way).wait_recv()
                if d + 1 < Z:
                    pl.when(can_send(d + 1, way))(lambda: zcopy(d + 1, way).start())
                spread(plane(d, way), zbufs[2 * (d - 1) + way])
        for way in (0, 1):
            pl.when(comes(d, way))(lambda d=d, way=way: compute(plane(d, way)))
        if d + 1 < Z:
            for way in (0, 1):
                start_chain(d, way)

    def ucopy(to, src):
        return far("item", to, us.at[to], ur.at[src], usend.at[to], urecv.at[src])

    for j in range(1, Z):
        to = lax.rem(z + j, Z)
        encode(us.at[to], ug[pl.ds(pl.multiple_of(to * piece, piece), piece), :], user_unit)
        ucopy(to, z).start()
    for way in (0, 1):
        start_chain(Z - 1, way)

    def vcopy(to, src, j):
        return far("item", to, ugs, ugr.at[src], vsend.at[j], vrecv.at[src])

    def share_users():
        total = ug[pl.ds(pl.multiple_of(z * piece, piece), piece), :]
        for j in range(1, Z):
            src = lax.rem(z + j, Z)
            ucopy(z, src).wait_recv()
            total = total + decode(ur.at[src], user_unit)
        encode(ugs, total, user_unit)
        for j in range(1, Z):
            vcopy(lax.rem(z + j, Z), z, j - 1).start()
        user_out[pl.ds(pl.multiple_of(z * piece, piece), piece), :] = decode(ugs, user_unit)

    inner = (z > 0) & (z < Z - 1)
    pl.when(inner)(lambda: [await_grads(lax.rem(z + j, Z)) for j in range(1, Z)] and None)

    def relay(r):
        def up(b):
            pl.when(z < r)(lambda: pass_on(r, b, 0, True))

        def down(b):
            pl.when(z > Z - 1 - r)(lambda: pass_on(Z - 1 - r, b, 1, True))

        def one(b, c):
            pl.when(2 * z < Z - 1)(lambda: up(b))
            down(b)
            pl.when(2 * z >= Z - 1)(lambda: up(b))
            return c
        lax.fori_loop(0, B // RUN, one, 0)

    for r in range(1, Z - 1):
        pl.when(inner)(lambda r=r: relay(r))
    pl.when(inner)(lambda: relay(Z - 1))
    share_users()

    await_grads(z)

    def finish(b, c):
        item_out[b] = dense(z, b)

        @pl.when(z > 0)
        def _():
            pl.when(lax.rem(b, RUN) == 0)(lambda: up_copy(z, z, b // RUN).wait_recv())
            item_out[b] += decode(cr.at[z, b], item_unit)

        @pl.when(z < Z - 1)
        def _():
            pl.when(lax.rem(b, RUN) == 0)(lambda: last_copy(z, z, b // RUN).wait_recv())
            item_out[b] += decode(crd.at[b], item_unit)
        return c

    lax.fori_loop(0, B, finish, 0)

    for j in range(1, Z):
        src = lax.rem(z + j, Z)
        vcopy(z, src, j - 1).wait_recv()
        user_out[pl.ds(pl.multiple_of(src * piece, piece), piece), :] = decode(ugr.at[src], user_unit)

    for d in range(1, Z):
        for way in (0, 1):
            pl.when(can_send(d, way))(lambda d=d, way=way: zcopy(d, way).wait_send())

    def drain(j, c):
        to = lax.rem(me + j, U)
        for p in range(Z):
            icopy(p, to, me).wait_send()
            gcopy(p, to, me).wait_send()
        return c

    lax.fori_loop(1, U, drain, 0)
    for j in range(1, Z):
        to = lax.rem(z + j, Z)
        ucopy(to, z).wait_send()
        vcopy(to, z, j - 1).wait_send()

        def drained(b, c):
            up_copy(z, to, b).wait_send()
            return c
        lax.fori_loop(0, B // RUN, drained, 0)


def exchange(pick, items, user, feedback, U, Z):
    B, T, K = items.shape
    N = user.shape[0]
    piece = N // Z
    coded = T + PAD
    dma = pltpu.SemaphoreType.DMA
    i16 = jnp.int16
    vmem = pl.BlockSpec(memory_space=pltpu.VMEM)
    return pl.pallas_call(
        functools.partial(kernel, U, Z),
        out_shape=(jax.ShapeDtypeStruct((B, T, K), jnp.float32), jax.ShapeDtypeStruct((N, K), jnp.float32)),
        in_specs=[pl.BlockSpec(memory_space=pltpu.SMEM), vmem, vmem, pl.BlockSpec(memory_space=pl.ANY)],
        out_specs=(vmem, vmem),
        scratch_shapes=[pltpu.VMEM((B, T, K), jnp.bfloat16)] * (2 * (Z - 1) + 1) + [
            pltpu.VMEM((N, K), jnp.bfloat16),
            pltpu.VMEM((Z, U, T, K), jnp.bfloat16),
            pltpu.VMEM((Z, U, T, K), jnp.bfloat16),
            pltpu.VMEM((Z, U, coded, K), i16),
            pltpu.VMEM((Z, U, coded, K), i16),
            pltpu.VMEM((Z, B, coded, K), i16),
            pltpu.VMEM((Z, B, coded, K), i16),
            pltpu.VMEM((B, coded, K), i16),
            pltpu.VMEM((2, 2, N, T), jnp.bfloat16),
            pltpu.VMEM((Z, piece + PAD, K), i16),
            pltpu.VMEM((Z, piece + PAD, K), i16),
            pltpu.VMEM((piece + PAD, K), i16),
            pltpu.VMEM((Z, piece + PAD, K), i16),
            pltpu.VMEM((N, K), jnp.float32),
            dma((2 * (Z - 1),)), dma((2 * (Z - 1),)),
            dma((Z, U)), dma((Z, U)), dma((Z, U)), dma((Z, U)),
            dma((Z, B // RUN)), dma((Z, B // RUN)), dma((B // RUN,)),
            dma((2,)),
            dma((Z,)), dma((Z,)), dma((Z,)), dma((Z,)),
        ],
        compiler_params=pltpu.CompilerParams(
            collective_id=0, has_side_effects=True, vmem_limit_bytes=63 * 2**20),
    )(pick, items, user, feedback)


def local(user_factors, item_factors, feedback, item_pick, user_noise, item_noise):
    U, Z = lax.axis_size("user"), lax.axis_size("item")
    tile, rank = feedback.shape[2], item_factors.shape[1]
    held = item_factors.shape[0] // tile
    items = item_factors.reshape(held, tile, rank)
    item_grad, user_grad = exchange(
        item_pick, items, user_factors,
        feedback.reshape(U, Z, feedback.shape[1], tile), U, Z)
    item_grad = item_grad.reshape(item_factors.shape)
    new_item = item_factors - item_step * (item_grad + prior_weight * item_factors) + item_noise_scale * item_noise
    new_user = user_factors - step_size * (user_grad + prior_weight * user_factors) + noise_scale * user_noise
    return (new_user, new_item)


def solution(mesh):
    in_specs = (
        P("user", None),
        P(("user", "item"), None),
        P("item", "user", None),
        P(),
        P("user", None),
        P(("user", "item"), None),
    )
    out_specs = (P("user", None), P(("user", "item"), None))
    return jax.shard_map(local, mesh=mesh, in_specs=in_specs, out_specs=out_specs, check_vma=False)
```

profile of v0, /device:TPU:0, one launch (start us, length us, event | category | flops | bytes accessed | tf_op | source)
XLA Modules:
  0.0 116.1 jit_solution(8673348716109480151)
XLA Ops:
  0.6 0.0 copy-start
  0.6 110.3 %shard_map.77 = (f32[8,128,256]{2,1,0:T(8,128)}, f32[512,256]{1,0:T(8,128)}) custom-call(s32[32,32]{1,0:T(8,128)} %pick.1, f32[8,128,256]{2,1,0:T(8,128)} %bitcast.11, f32[512,256]{1,0:T(8,128)} %user_wide.1, bf16[8,4,512,128]{3,2,1,0:T(8,128)(2,1)} %bitcast.10), custom_call_target="tpu_custom_call" | custom-call | tf_op jit(solution)/shard_map/pallas_call | solution.py:322
  111.0 0.0 copy-done
  111.0 2.1 %multiply_add_fusion = f32[512,256]{1,0:T(8,128)} fusion(f32[512,256]{1,0:T(8,128)} %param.10, f32[512,256]{1,0:T(8,128)S(1)} %copy-done, f32[512,256]{1,0:T(8,128)} %get-tuple-element.4), kind=kLoop, calls=%fused_computation.4 | loop fusion | flops 655360 | bytes 2097152 | tf_op jit(solution)/shard_map/add | solution.py:363
  113.1 3.0 %fusion.2 = f32[1024,256]{1,0:T(8,128)} fusion(f32[1024,256]{1,0:T(8,128)} %param.7, f32[8,128,256]{2,1,0:T(8,128)} %get-tuple-element.5, f32[1024,256]{1,0:T(8,128)} %param.11), kind=kLoop, calls=%fused_computation.3 | loop fusion | flops 1310720 | bytes 4194304 | tf_op jit(solution)/shard_map/add | solution.py:362
Async XLA Ops:
  0.6 110.3 %copy-start = (f32[512,256]{1,0:T(8,128)S(1)}, f32[512,256]{1,0:T(8,128)}, u32[]{:S(2)}) copy-start(f32[512,256]{1,0:T(8,128)} %user_wide.1) | copy-start | bytes 1572868
where the time goes:
time: 116 us
  Pallas kernels  110 us (95%)
  other arithmetic  5.13 us (4%)
    pallas_call x1, Pallas kernels, exchange(): pl.pallas_call(functools.partial(kernel, U, Z), out_shape=(jax.ShapeDtype...  110 us
    add x1, other arithmetic, local(): item_factors - item_step * (item_grad + prior_weight * item_factors)  3.03 us

commit v1 on v0

v1 whole, which is shorter than its diff:
```python
import functools
import math

import jax
import jax.numpy as jnp
from jax import lax
from jax.experimental import pallas as pl
from jax.experimental.pallas import tpu as pltpu
from jax.sharding import PartitionSpec as P

step_size = 0.01
item_step = 0.1
prior_weight = 1.0
noise_scale = math.sqrt(0.02)
item_noise_scale = math.sqrt(0.2)

FACTOR_BOUND = 1.5
LEVELS = 32766.0
HALVES = 2
RUN = 4
PAD = 8


def encode(ref, value, unit):
    rows = value.shape[0]
    largest = jnp.max(jnp.abs(value), axis=0, keepdims=True)
    count = jnp.floor(largest * (1.0 / (LEVELS * unit))) + 1.0
    inverse = 1.0 / (count * unit)
    ref[pl.ds(0, rows), :] = jnp.round(value * inverse).astype(jnp.int32).astype(jnp.int16)
    ref[pl.ds(rows, PAD), :] = jnp.broadcast_to(count, (PAD, value.shape[1])).astype(jnp.int32).astype(jnp.int16)


def decode(ref, weight, start=0, size=None):
    rows = ref.shape[0] - PAD
    size = rows if size is None else size
    count = ref[pl.ds(rows, PAD), :].astype(jnp.float32)[0:1]
    return ref[pl.ds(start, size), :].astype(jnp.float32) * (count * weight)


def kernel(
    U, Z, H, pick, items_wide, user_wide, feedback, item_out, user_out, *scratch
):
    held = scratch[:H]
    zbufs = scratch[H: H + 2 * (Z - 1) * H]
    (user, og, arr, gs, gr, cs, cr, crd, fb, us, ur, ugs, ugr, ug, values, sums, zsend, zrecv, isend, irecv, gsend,
     grecv, csend, crecv, cdrecv, fsem, usend, urecv, vsend, vrecv) = scratch[H + 2 * (Z - 1) * H:]
    B, T, K = items_wide.shape
    R = T // H
    N = user.shape[0]
    G = fb.shape[1]
    groups = U // G
    piece = N // Z
    runs = B // RUN
    me = lax.axis_index("user")
    z = lax.axis_index("item")
    item_unit = N * FACTOR_BOUND * U / LEVELS / 32000.0
    user_unit = U * Z * T * FACTOR_BOUND * Z / LEVELS / 32000.0

    def far(axis, to, src, dst, ssem, rsem):
        return pltpu.make_async_remote_copy(
            src_ref=src, dst_ref=dst, send_sem=ssem, recv_sem=rsem,
            device_id={axis: to}, device_id_type=pl.DeviceIdType.MESH)

    barrier = pltpu.get_barrier_semaphore()

    def greet_user(j, c):
        pl.semaphore_signal(barrier, inc=1, device_id={"user": lax.rem(me + j, U)}, device_id_type=pl.DeviceIdType.MESH)
        return c

    lax.fori_loop(1, U, greet_user, 0)
    for j in range(1, Z):
        pl.semaphore_signal(barrier, inc=1, device_id={"item": lax.rem(z + j, Z)}, device_id_type=pl.DeviceIdType.MESH)

    def rows_of(h):
        return pl.ds(pl.multiple_of(lax.rem(me + h, H) * R, R), R)

    for h in range(H):
        held[h][...] = items_wide[:, rows_of(h), :].astype(jnp.bfloat16)

    pl.semaphore_wait(barrier, U - 1 + Z - 1)

    def zbuf(d, way, h):
        return held[h] if d == 0 else zbufs[(2 * (d - 1) + way) * H + h]

    def zcopy(d, way, h):
        k = (2 * (d - 1) + way) * H + h
        return far("item", z + (1 if way == 0 else -1), zbuf(d - 1, way, h), zbuf(d, way, h), zsend.at[k], zrecv.at[k])

    def can_send(d, way):
        return (z - (d - 1) >= 0) & (z + 1 < Z) if way == 0 else (z + (d - 1) < Z) & (z >= 1)

    def comes(d, way):
        return z - d >= 0 if way == 0 else z + d < Z

    for h in range(H):
        for way in (0, 1):
            pl.when(can_send(1, way))(lambda way=way, h=h: zcopy(1, way, h).start())

    user[...] = user_wide[...].astype(jnp.bfloat16)

    def slot_of(o, h):
        return o // H * H + lax.rem(o + h, H)

    def owner_of(j, h):
        return j // H * H + lax.rem(j + H - h, H)

    def icopy(p, h, to, src):
        return far("user", to, og.at[p, h, to], arr.at[p, h, slot_of(src, h)], isend.at[p, h, to], irecv.at[p, h, src])

    def spread(p, h, blocks):
        def one(j, c):
            to = lax.rem(me + j, U)
            og[p, h, to] = blocks[pick[to * Z + z, me * Z + p]]
            icopy(p, h, to, me).start()
            return c
        lax.fori_loop(1, U, one, 0)
        arr[p, h, slot_of(me, h)] = blocks[pick[me * Z + z, me * Z + p]]

    def gcopy(p, h, to, src):
        return far("user", to, gs.at[p, h, to], gr.at[p, h, src], gsend.at[p, h, to], grecv.at[p, h, src])

    def fcopy(p, g, at):
        return pltpu.make_async_copy(feedback.at[pl.ds(G * g, G), p], fb.at[at], fsem.at[at])

    lane = lax.broadcasted_iota(jnp.int32, (N, T), 1)

    def group_of(j):
        return lax.rem(me // G + groups - j, groups)

    def compute(p, h, send):
        fcopy(p, group_of(0), 0).start()

        def one(j, c):
            g = group_of(j)
            at = lax.rem(j, 2)

            @pl.when(j + 1 < groups)
            def _():
                fcopy(p, group_of(j + 1), 1 - at).start()

            def arrive(t, c):
                o = G * g + t
                pl.when(o != me)(lambda: icopy(p, h, me, o).wait_recv())
                return c

            lax.fori_loop(0, G, arrive, 0)
            fcopy(p, g, at).wait()
            tile = arr[p, h, pl.ds(G * g, G)].reshape(G * R, K)
            scores = lax.dot_general(user[...], tile, (((1,), (1,)), ((), ())), preferred_element_type=jnp.float32)
            target = []
            for m in range(G // H):
                lanes = fb[at, m * H + owner_of(H - 1, h)]
                for s in range(H - 1):
                    lanes = jnp.where((lane >= s * R) & (lane < (s + 1) * R), fb[at, m * H + owner_of(s, h)], lanes)
                target.append(lanes)
            target = jnp.concatenate(target, axis=1).astype(jnp.float32)
            residual = (0.5 * jnp.tanh(0.5 * scores) + (0.5 - target)).astype(jnp.bfloat16)
            part = lax.dot_general(residual, user[...], (((0,), (0,)), ((), ())), preferred_element_type=jnp.float32)
            for t in range(G):
                o = owner_of(G * g + t, h)
                encode(gs.at[p, h, o], part[t * R:(t + 1) * R], item_unit)

                @pl.when(o == me)
                def _():
                    gr[p, h, me] = gs[p, h, me]

                if send:
                    pl.when(o != me)(lambda: gcopy(p, h, o, me).start())
            ug[...] += jnp.dot(residual, tile, preferred_element_type=jnp.float32)
            return c

        lax.fori_loop(0, groups, one, 0)

    def collect(p, h, way):
        def one(j, c):
            u = lax.rem(me + j, U)
            pl.when(j > 0)(lambda: gcopy(p, h, me, u).wait_recv())
            values[way, u] = decode(gr.at[p, h, u], item_unit)
            return c
        lax.fori_loop(0, U, one, 0)

    def dense(p, b, way):
        def one(u, acc):
            weight = jnp.where(pick[u * Z + z, me * Z + p] == b, 1.0, 0.0).astype(jnp.float32)
            return acc + values[way, u] * weight
        return lax.fori_loop(0, U, one, jnp.zeros((R, K), jnp.float32), unroll=8)

    def up_copy(to, p, h, c):
        return far("item", to, cs.at[p, h, c], cr.at[p, h, c], csend.at[p, h, c], crecv.at[p, h, c])

    def last_copy(to, p, h, c):
        return far("item", to, cs.at[p, h, c], crd.at[h, c], csend.at[p, h, c], cdrecv.at[h, c])

    def phase(r, h):
        def target(way):
            return r + way * (Z - 1 - 2 * r)

        def active(way):
            return (way == 0) & (z < r) | (way == 1) & (z > Z - 1 - r)

        def source(way):
            return (way == 0) & (z == 0) | (way == 1) & (z == Z - 1)

        for way in (0, 1):
            pl.when(active(way))(lambda way=way: collect(target(way), h, way))

        def pass_on(c, way):
            p = target(way)
            to = z + 1 - 2 * way
            relay = jnp.logical_not(source(way))
            pl.when(relay)(lambda: up_copy(z, p, h, c).wait_recv())

            def one(i, carry):
                at = pl.ds(pl.multiple_of(i * R, R), R)
                sums[at, :] = dense(p, c * RUN + i, way)

                @pl.when(relay)
                def _():
                    sums[at, :] += decode(cr.at[p, h, c], item_unit, pl.multiple_of(i * R, R), R)
                return carry
            lax.fori_loop(0, RUN, one, 0)
            encode(cs.at[p, h, c], sums[...], item_unit)
            last = (way == 1) & (to == p)
            pl.when(last)(lambda: last_copy(to, p, h, c).start())
            pl.when(jnp.logical_not(last))(lambda: up_copy(to, p, h, c).start())

        def one(k, carry):
            c = k // 2
            low = jnp.where(2 * z < Z - 1, 1, 0)
            way = lax.rem(k + 1 - low, 2)
            pl.when(active(way))(lambda: pass_on(c, way))
            return carry
        lax.fori_loop(0, 2 * runs, one, 0)

    def ucopy(to, src):
        return far("item", to, us.at[to], ur.at[src], usend.at[to], urecv.at[src])

    def plane(d, way):
        return z - d if way == 0 else z + d

    def own_out():
        for h in range(H):
            def one(j, c):
                gcopy(z, h, lax.rem(me + j, U), me).start()
                return c
            lax.fori_loop(1, U, one, 0)
        for j in range(1, Z):
            to = lax.rem(z + j, Z)
            encode(us.at[to], ug[pl.ds(pl.multiple_of(to * piece, piece), piece), :], user_unit)
            ucopy(to, z).start()

    with jax.named_scope("spread_own"):
        for h in range(H):
            spread(z, h, held[h])
    ug[...] = jnp.zeros_like(ug)

    with jax.named_scope("compute_own"):
        def own(h, c):
            compute(z, h, False)
            return c
        lax.fori_loop(0, H, own, 0)

    farthest = jnp.maximum(z, Z - 1 - z)

    def step(s, carry):
        d = s // H + 1
        h = lax.rem(s, H)
        with jax.named_scope("arrive"):
            for e in range(1, Z):
                for way in (0, 1):
                    for f in range(H):
                        @pl.when(comes(e, way) & (s == (e - 1) * H + f))
                        def _(e=e, way=way, f=f):
                            zcopy(e, way, f).wait_recv()
                            if e + 1 < Z:
                                pl.when(can_send(e + 1, way))(lambda: zcopy(e + 1, way, f).start())
                            spread(plane(e, way), f, zbuf(e, way, f))
        with jax.named_scope("compute"):
            for way in (0, 1):
                pl.when(comes(d, way))(lambda way=way: compute(plane(d, way), h, True))
        with jax.named_scope("own_out"):
            pl.when((d == farthest) & (h == H - 1))(own_out)
        with jax.named_scope("phase"):
            pl.when(s > 0)(lambda: phase((s - 1) // H + 1, lax.rem(s - 1, H)))
        return carry

    steps = (Z - 1) * H
    lax.fori_loop(0, steps, step, 0)
    with jax.named_scope("lastphase"):
        phase(Z - 1, H - 1)

    def vcopy(to, src, j):
        return far("item", to, ugs, ugr.at[src], vsend.at[j], vrecv.at[src])

    def share_users():
        total = ug[pl.ds(pl.multiple_of(z * piece, piece), piece), :]
        for j in range(1, Z):
            src = lax.rem(z + j, Z)
            ucopy(z, src).wait_recv()
            total = total + decode(ur.at[src], user_unit)
        encode(ugs, total, user_unit)
        for j in range(1, Z):
            vcopy(lax.rem(z + j, Z), z, j - 1).start()
        user_out[pl.ds(pl.multiple_of(z * piece, piece), piece), :] = decode(ugs, user_unit)

    with jax.named_scope("share"):
        share_users()

    def finish(h, carry):
        collect(z, h, 0)
        rows = rows_of(h)

        def one(b, carry):
            c = b // RUN
            at = pl.multiple_of(lax.rem(b, RUN) * R, R)
            item_out[b, rows, :] = dense(z, b, 0)

            @pl.when(z > 0)
            def _():
                pl.when(lax.rem(b, RUN) == 0)(lambda: up_copy(z, z, h, c).wait_recv())
                item_out[b, rows, :] += decode(cr.at[z, h, c], item_unit, at, R)

            @pl.when(z < Z - 1)
            def _():
                pl.when(lax.rem(b, RUN) == 0)(lambda: last_copy(z, z, h, c).wait_recv())
                item_out[b, rows, :] += decode(crd.at[h, c], item_unit, at, R)
            return carry

        lax.fori_loop(0, B, one, 0)
        return carry

    with jax.named_scope("finish"):
        lax.fori_loop(0, H, finish, 0)

    with jax.named_scope("userout"):
        for j in range(1, Z):
            src = lax.rem(z + j, Z)
            vcopy(z, src, j - 1).wait_recv()
            user_out[pl.ds(pl.multiple_of(src * piece, piece), piece), :] = decode(ugr.at[src], user_unit)

    for d in range(1, Z):
        for way in (0, 1):
            for h in range(H):
                pl.when(can_send(d, way))(lambda d=d, way=way, h=h: zcopy(d, way, h).wait_send())

    def drain(j, c):
        to = lax.rem(me + j, U)

        def one(k, c):
            icopy(k // H, lax.rem(k, H), to, me).wait_send()
            gcopy(k // H, lax.rem(k, H), to, me).wait_send()
            return c
        return lax.fori_loop(0, Z * H, one, c)

    lax.fori_loop(1, U, drain, 0)
    for j in range(1, Z):
        to = lax.rem(z + j, Z)
        ucopy(to, z).wait_send()
        vcopy(to, z, j - 1).wait_send()

        def drained(k, c):
            up_copy(z, to, k // runs, lax.rem(k, runs)).wait_send()
            return c
        lax.fori_loop(0, H * runs, drained, 0)


def exchange(pick, items, user, feedback, U, Z):
    B, T, K = items.shape
    N = user.shape[0]
    H = HALVES
    R = T // H
    G = min(U, 2 * H)
    piece = N // Z
    runs = B // RUN
    dma = pltpu.SemaphoreType.DMA
    i16 = jnp.int16
    bf16 = jnp.bfloat16
    vmem = pl.BlockSpec(memory_space=pltpu.VMEM)
    return pl.pallas_call(
        functools.partial(kernel, U, Z, H),
        out_shape=(jax.ShapeDtypeStruct((B, T, K), jnp.float32), jax.ShapeDtypeStruct((N, K), jnp.float32)),
        in_specs=[pl.BlockSpec(memory_space=pltpu.SMEM), vmem, vmem, pl.BlockSpec(memory_space=pl.ANY)],
        out_specs=(vmem, vmem),
        scratch_shapes=[pltpu.VMEM((B, R, K), bf16)] * (H * (2 * (Z - 1) + 1)) + [
            pltpu.VMEM((N, K), bf16),
            pltpu.VMEM((Z, H, U, R, K), bf16),
            pltpu.VMEM((Z, H, U, R, K), bf16),
            pltpu.VMEM((Z, H, U, R + PAD, K), i16),
            pltpu.VMEM((Z, H, U, R + PAD, K), i16),
            pltpu.VMEM((Z, H, runs, RUN * R + PAD, K), i16),
            pltpu.VMEM((Z, H, runs, RUN * R + PAD, K), i16),
            pltpu.VMEM((H, runs, RUN * R + PAD, K), i16),
            pltpu.VMEM((2, G, N, T), bf16),
            pltpu.VMEM((Z, piece + PAD, K), i16),
            pltpu.VMEM((Z, piece + PAD, K), i16),
            pltpu.VMEM((piece + PAD, K), i16),
            pltpu.VMEM((Z, piece + PAD, K), i16),
            pltpu.VMEM((N, K), jnp.float32),
            pltpu.VMEM((2, U, R, K), jnp.float32),
            pltpu.VMEM((RUN * R, K), jnp.float32),
            dma((2 * (Z - 1) * H,)), dma((2 * (Z - 1) * H,)),
            dma((Z, H, U)), dma((Z, H, U)), dma((Z, H, U)), dma((Z, H, U)),
            dma((Z, H, runs)), dma((Z, H, runs)), dma((H, runs)),
            dma((2,)),
            dma((Z,)), dma((Z,)), dma((Z,)), dma((Z,)),
        ],
        compiler_params=pltpu.CompilerParams(
            collective_id=0, has_side_effects=True, vmem_limit_bytes=63 * 2**20),
    )(pick, items, user, feedback)


def local(user_factors, item_factors, feedback, item_pick, user_noise, item_noise):
    U, Z = lax.axis_size("user"), lax.axis_size("item")
    tile, rank = feedback.shape[2], item_factors.shape[1]
    held = item_factors.shape[0] // tile
    items = item_factors.reshape(held, tile, rank)
    item_grad, user_grad = exchange(
        item_pick, items, user_factors,
        feedback.reshape(U, Z, feedback.shape[1], tile), U, Z)
    item_grad = item_grad.reshape(item_factors.shape)
    new_item = item_factors - item_step * (item_grad + prior_weight * item_factors) + item_noise_scale * item_noise
    new_user = user_factors - step_size * (user_grad + prior_weight * user_factors) + noise_scale * user_noise
    return (new_user, new_item)


def solution(mesh):
    in_specs = (
        P("user", None),
        P(("user", "item"), None),
        P("item", "user", None),
        P(),
        P("user", None),
        P(("user", "item"), None),
    )
    out_specs = (P("user", None), P(("user", "item"), None))
    return jax.shard_map(local, mesh=mesh, in_specs=in_specs, out_specs=out_specs, check_vma=False)
```

time: 116 us -> 116 us (level)
  no operation moved by 1% of the time
where the time goes in v1:
time: 116 us
  Pallas kernels  110 us (95%)
  other arithmetic  5.13 us (4%)
    pallas_call x1, Pallas kernels, exchange(): pl.pallas_call(functools.partial(kernel, U, Z, H), out_shape=(jax.ShapeDt...  110 us
    add x1, other arithmetic, local(): item_factors - item_step * (item_grad + prior_weight * item_factors)  3.03 us

profile of v1, /device:TPU:0, one launch (start us, length us, event | category | flops | bytes accessed | tf_op | source)
XLA Modules:
  0.0 116.1 jit_solution(8014391147186567938)
XLA Ops:
  0.6 0.0 copy-start
  0.6 110.3 %shard_map.77 = (f32[8,128,256]{2,1,0:T(8,128)}, f32[512,256]{1,0:T(8,128)}) custom-call(s32[32,32]{1,0:T(8,128)} %pick.1, f32[8,128,256]{2,1,0:T(8,128)} %bitcast.11, f32[512,256]{1,0:T(8,128)} %user_wide.1, bf16[8,4,512,128]{3,2,1,0:T(8,128)(2,1)} %bitcast.10), custom_call_target="tpu_custom_call" | custom-call | tf_op jit(solution)/shard_map/pallas_call | solution.py:379
  110.9 0.0 copy-done
  110.9 2.1 %multiply_add_fusion = f32[512,256]{1,0:T(8,128)} fusion(f32[512,256]{1,0:T(8,128)} %param.10, f32[512,256]{1,0:T(8,128)S(1)} %copy-done, f32[512,256]{1,0:T(8,128)} %get-tuple-element.4), kind=kLoop, calls=%fused_computation.4 | loop fusion | flops 655360 | bytes 2097152 | tf_op jit(solution)/shard_map/add | solution.py:422
  113.0 3.0 %fusion.2 = f32[1024,256]{1,0:T(8,128)} fusion(f32[1024,256]{1,0:T(8,128)} %param.7, f32[8,128,256]{2,1,0:T(8,128)} %get-tuple-element.5, f32[1024,256]{1,0:T(8,128)} %param.11), kind=kLoop, calls=%fused_computation.3 | loop fusion | flops 1310720 | bytes 4194304 | tf_op jit(solution)/shard_map/add | solution.py:421
Async XLA Ops:
  0.6 110.3 %copy-start = (f32[512,256]{1,0:T(8,128)S(1)}, f32[512,256]{1,0:T(8,128)}, u32[]{:S(2)}) copy-start(f32[512,256]{1,0:T(8,128)} %user_wide.1) | copy-start | bytes 1572868

commit v2 on v1

--- a/solution.py
+++ b/solution.py
@@ -19,6 +19,7 @@
 HALVES = 2
 RUN = 4
 PAD = 8
+PIECES = 4
 
 
 def encode(ref, value, unit):
@@ -42,14 +43,14 @@
 ):
     held = scratch[:H]
     zbufs = scratch[H: H + 2 * (Z - 1) * H]
-    (user, og, arr, gs, gr, cs, cr, crd, fb, us, ur, ugs, ugr, ug, values, sums, zsend, zrecv, isend, irecv, gsend,
-     grecv, csend, crecv, cdrecv, fsem, usend, urecv, vsend, vrecv) = scratch[H + 2 * (Z - 1) * H:]
+    (user, og, arr, gs, gr, cs, cr, crd, fb, us, ur, xr, ws, wr, ug, values, sums, zsend, zrecv, isend, irecv, gsend,
+     grecv, csend, crecv, cdrecv, fsem, usend, urecv, xrecv, wsend, wrecv) = scratch[H + 2 * (Z - 1) * H:]
     B, T, K = items_wide.shape
     R = T // H
     N = user.shape[0]
     G = fb.shape[1]
     groups = U // G
-    piece = N // Z
+    piece = N // PIECES
     runs = B // RUN
     me = lax.axis_index("user")
     z = lax.axis_index("item")
@@ -127,16 +128,14 @@
     def group_of(j):
         return lax.rem(me // G + groups - j, groups)
 
-    def compute(p, h, send):
-        fcopy(p, group_of(0), 0).start()
-
+    def prefetch(p, way):
+        for j in range(min(2, groups)):
+            fcopy(p, group_of(j), 2 * way + j).start()
+
+    def compute(p, h, way, send):
         def one(j, c):
             g = group_of(j)
-            at = lax.rem(j, 2)
-
-            @pl.when(j + 1 < groups)
-            def _():
-                fcopy(p, group_of(j + 1), 1 - at).start()
+            at = 2 * way + lax.rem(j, 2)
 
             def arrive(t, c):
                 o = G * g + t
@@ -167,6 +166,7 @@
                 if send:
                     pl.when(o != me)(lambda: gcopy(p, h, o, me).start())
             ug[...] += jnp.dot(residual, tile, preferred_element_type=jnp.float32)
+            pl.when(j + 2 < groups)(lambda: fcopy(p, group_of(j + 2), at).start())
             return c
 
         lax.fori_loop(0, groups, one, 0)
@@ -191,7 +191,7 @@
     def last_copy(to, p, h, c):
         return far("item", to, cs.at[p, h, c], crd.at[h, c], csend.at[p, h, c], cdrecv.at[h, c])
 
-    def phase(r, h):
+    def phase(r, h, begin, end):
         def target(way):
             return r + way * (Z - 1 - 2 * r)
 
@@ -201,8 +201,14 @@
         def source(way):
             return (way == 0) & (z == 0) | (way == 1) & (z == Z - 1)
 
-        for way in (0, 1):
-            pl.when(active(way))(lambda way=way: collect(target(way), h, way))
+        def in_turn(k):
+            return lax.rem(k + jnp.where(2 * z < Z - 1, 0, 1), 2)
+
+        def gather(k, carry):
+            way = in_turn(k)
+            pl.when(active(way))(lambda: collect(target(way), h, way))
+            return carry
+        lax.fori_loop(begin, end, gather, 0)
 
         def pass_on(c, way):
             p = target(way)
@@ -225,15 +231,10 @@
             pl.when(jnp.logical_not(last))(lambda: up_copy(to, p, h, c).start())
 
         def one(k, carry):
-            c = k // 2
-            low = jnp.where(2 * z < Z - 1, 1, 0)
-            way = lax.rem(k + 1 - low, 2)
-            pl.when(active(way))(lambda: pass_on(c, way))
+            way = in_turn(k // runs)
+            pl.when(active(way))(lambda: pass_on(lax.rem(k, runs), way))
             return carry
-        lax.fori_loop(0, 2 * runs, one, 0)
-
-    def ucopy(to, src):
-        return far("item", to, us.at[to], ur.at[src], usend.at[to], urecv.at[src])
+        lax.fori_loop(begin * runs, end * runs, one, 0)
 
     def plane(d, way):
         return z - d if way == 0 else z + d
@@ -244,10 +245,17 @@
                 gcopy(z, h, lax.rem(me + j, U), me).start()
                 return c
             lax.fori_loop(1, U, one, 0)
-        for j in range(1, Z):
-            to = lax.rem(z + j, Z)
-            encode(us.at[to], ug[pl.ds(pl.multiple_of(to * piece, piece), piece), :], user_unit)
-            ucopy(to, z).start()
+
+    def arrive(s):
+        for e in range(1, Z):
+            for way in (0, 1):
+                for f in range(H):
+                    @pl.when(comes(e, way) & (s == (e - 1) * H + f))
+                    def _(e=e, way=way, f=f):
+                        zcopy(e, way, f).wait_recv()
+                        if e + 1 < Z:
+                            pl.when(can_send(e + 1, way))(lambda: zcopy(e + 1, way, f).start())
+                        spread(plane(e, way), f, zbuf(e, way, f))
 
     with jax.named_scope("spread_own"):
         for h in range(H):
@@ -256,55 +264,102 @@
 
     with jax.named_scope("compute_own"):
         def own(h, c):
-            compute(z, h, False)
+            prefetch(z, 0)
+            compute(z, h, 0, False)
+            pl.when(h == 0)(lambda: arrive(h))
             return c
         lax.fori_loop(0, H, own, 0)
 
+    edge = (z == 0) | (z == Z - 1)
     farthest = jnp.maximum(z, Z - 1 - z)
+    steps = (Z - 1) * H
 
     def step(s, carry):
         d = s // H + 1
         h = lax.rem(s, H)
+        for way in (0, 1):
+            pl.when(comes(d, way))(lambda way=way: prefetch(plane(d, way), way))
         with jax.named_scope("arrive"):
-            for e in range(1, Z):
-                for way in (0, 1):
-                    for f in range(H):
-                        @pl.when(comes(e, way) & (s == (e - 1) * H + f))
-                        def _(e=e, way=way, f=f):
-                            zcopy(e, way, f).wait_recv()
-                            if e + 1 < Z:
-                                pl.when(can_send(e + 1, way))(lambda: zcopy(e + 1, way, f).start())
-                            spread(plane(e, way), f, zbuf(e, way, f))
+            arrive(s + 1)
         with jax.named_scope("compute"):
             for way in (0, 1):
-                pl.when(comes(d, way))(lambda way=way: compute(plane(d, way), h, True))
+                pl.when(comes(d, way))(lambda way=way: compute(plane(d, way), h, way, True))
         with jax.named_scope("own_out"):
-            pl.when((d == farthest) & (h == H - 1))(own_out)
+            pl.when(jnp.logical_not(edge) & (d == farthest) & (h == H - 1))(own_out)
         with jax.named_scope("phase"):
-            pl.when(s > 0)(lambda: phase((s - 1) // H + 1, lax.rem(s - 1, H)))
+            ready = s - jnp.where(edge, 1, 0)
+            pl.when((ready >= 0) & (ready < (Z - 2) * H))(lambda: phase(ready // H + 1, lax.rem(ready, H), 0, 2))
         return carry
 
-    steps = (Z - 1) * H
     lax.fori_loop(0, steps, step, 0)
-    with jax.named_scope("lastphase"):
-        phase(Z - 1, H - 1)
-
-    def vcopy(to, src, j):
-        return far("item", to, ugs, ugr.at[src], vsend.at[j], vrecv.at[src])
-
-    def share_users():
-        total = ug[pl.ds(pl.multiple_of(z * piece, piece), piece), :]
-        for j in range(1, Z):
-            src = lax.rem(z + j, Z)
-            ucopy(z, src).wait_recv()
-            total = total + decode(ur.at[src], user_unit)
-        encode(ugs, total, user_unit)
-        for j in range(1, Z):
-            vcopy(lax.rem(z + j, Z), z, j - 1).start()
-        user_out[pl.ds(pl.multiple_of(z * piece, piece), piece), :] = decode(ugs, user_unit)
-
-    with jax.named_scope("share"):
-        share_users()
+
+    half = Z // 2
+    inward = jnp.where(z < half, 1, -1)
+    middle = (z == half - 1) | (z == half)
+
+    def in_copy(to, q):
+        return far("item", to, us.at[q], ur.at[q], usend.at[q], urecv.at[q])
+
+    def cross_copy(to, q):
+        return far("item", to, us.at[q], xr.at[q], usend.at[q], xrecv.at[q])
+
+    def out_copy(src, to, q):
+        return far("item", to, src.at[q], wr.at[q], wsend.at[q], wrecv.at[q])
+
+    def rows_q(q):
+        return pl.ds(pl.multiple_of(q * piece, piece), piece)
+
+    def users_in(q, carry):
+        rows = rows_q(q)
+
+        @pl.when(jnp.logical_not(edge))
+        def _():
+            in_copy(z, q).wait_recv()
+            ug[rows, :] += decode(ur.at[q], user_unit)
+        encode(us.at[q], ug[rows, :], user_unit)
+        pl.when(middle)(lambda: cross_copy(z + inward, q).start())
+        pl.when(jnp.logical_not(middle))(lambda: in_copy(z + inward, q).start())
+        return carry
+
+    def users_out(q, carry):
+        rows = rows_q(q)
+
+        @pl.when(middle)
+        def _():
+            cross_copy(z, q).wait_recv()
+            encode(ws.at[q], decode(us.at[q], user_unit) + decode(xr.at[q], user_unit), user_unit)
+            pl.when(jnp.logical_not(edge))(lambda: out_copy(ws, z - inward, q).start())
+            user_out[rows, :] = decode(ws.at[q], user_unit)
+
+        @pl.when(jnp.logical_not(middle))
+        def _():
+            out_copy(ws, z, q).wait_recv()
+            pl.when(jnp.logical_not(edge))(lambda: out_copy(wr, z - inward, q).start())
+            user_out[rows, :] = decode(wr.at[q], user_unit)
+        return carry
+
+    def users_back():
+        lax.fori_loop(0, PIECES, users_out, 0)
+
+    def last_phase(first, last, k):
+        def one(h, c):
+            phase(Z - 1, h, k, k + 1)
+            return c
+        lax.fori_loop(first, last, one, 0)
+
+    with jax.named_scope("users_in"):
+        lax.fori_loop(0, PIECES, users_in, 0)
+    with jax.named_scope("phase_a"):
+        last_phase(0, H - 1, 0)
+    with jax.named_scope("users_mid"):
+        pl.when(middle)(users_back)
+    with jax.named_scope("phase_b"):
+        last_phase(0, H - 1, 1)
+    with jax.named_scope("phase_c"):
+        last_phase(H - 1, H, 0)
+    pl.when(edge)(own_out)
+    with jax.named_scope("phase_d"):
+        last_phase(H - 1, H, 1)
 
     def finish(h, carry):
         collect(z, h, 0)
@@ -333,10 +388,7 @@
         lax.fori_loop(0, H, finish, 0)
 
     with jax.named_scope("userout"):
-        for j in range(1, Z):
-            src = lax.rem(z + j, Z)
-            vcopy(z, src, j - 1).wait_recv()
-            user_out[pl.ds(pl.multiple_of(src * piece, piece), piece), :] = decode(ugr.at[src], user_unit)
+        pl.when(jnp.logical_not(middle))(users_back)
 
     for d in range(1, Z):
         for way in (0, 1):
@@ -355,13 +407,13 @@
     lax.fori_loop(1, U, drain, 0)
     for j in range(1, Z):
         to = lax.rem(z + j, Z)
-        ucopy(to, z).wait_send()
-        vcopy(to, z, j - 1).wait_send()
-
         def drained(k, c):
             up_copy(z, to, k // runs, lax.rem(k, runs)).wait_send()
             return c
         lax.fori_loop(0, H * runs, drained, 0)
+    for q in range(PIECES):
+        in_copy(z + inward, q).wait_send()
+        pl.when(jnp.logical_not(edge))(lambda q=q: out_copy(ws, z - inward, q).wait_send())
 
 
 def exchange(pick, items, user, feedback, U, Z):
@@ -370,7 +422,7 @@
     H = HALVES
     R = T // H
     G = min(U, 2 * H)
-    piece = N // Z
+    piece = N // PIECES
     runs = B // RUN
     dma = pltpu.SemaphoreType.DMA
     i16 = jnp.int16
@@ -390,19 +442,16 @@
             pltpu.VMEM((Z, H, runs, RUN * R + PAD, K), i16),
             pltpu.VMEM((Z, H, runs, RUN * R + PAD, K), i16),
             pltpu.VMEM((H, runs, RUN * R + PAD, K), i16),
-            pltpu.VMEM((2, G, N, T), bf16),
-            pltpu.VMEM((Z, piece + PAD, K), i16),
-            pltpu.VMEM((Z, piece + PAD, K), i16),
-            pltpu.VMEM((piece + PAD, K), i16),
-            pltpu.VMEM((Z, piece + PAD, K), i16),
+            pltpu.VMEM((4, G, N, T), bf16),
+        ] + [pltpu.VMEM((PIECES, piece + PAD, K), i16)] * 5 + [
             pltpu.VMEM((N, K), jnp.float32),
             pltpu.VMEM((2, U, R, K), jnp.float32),
             pltpu.VMEM((RUN * R, K), jnp.float32),
             dma((2 * (Z - 1) * H,)), dma((2 * (Z - 1) * H,)),
             dma((Z, H, U)), dma((Z, H, U)), dma((Z, H, U)), dma((Z, H, U)),
             dma((Z, H, runs)), dma((Z, H, runs)), dma((H, runs)),
-            dma((2,)),
-            dma((Z,)), dma((Z,)), dma((Z,)), dma((Z,)),
+            dma((4,)),
+            dma((PIECES,)), dma((PIECES,)), dma((PIECES,)), dma((PIECES,)), dma((PIECES,)),
         ],
         compiler_params=pltpu.CompilerParams(
             collective_id=0, has_side_effects=True, vmem_limit_bytes=63 * 2**20),

time: 116 us -> 96.3 us (0.83)
  Pallas kernels: 110 us -> 90.2 us
    pallas_call x1, Pallas kernels: 110 us -> 90.2 us  [exchange(): pl.pallas_call(functools.partial(kernel, U, Z, H), out_shape=(jax.ShapeDt...]
where the time goes in v2:
time: 96.3 us; the launch traced here: 96 us
  Pallas kernels  90.2 us (94%)
  other arithmetic  5.13 us (5%)
    pallas_call x1, Pallas kernels, exchange(): pl.pallas_call(functools.partial(kernel, U, Z, H), out_shape=(jax.ShapeDt...  90.2 us
    add x1, other arithmetic, local(): item_factors - item_step * (item_grad + prior_weight * item_factors)  3.03 us
    add x1, other arithmetic, local(): user_factors - step_size * (user_grad + prior_weight * user_factors)  2.1 us

profile of v2, /device:TPU:0, one launch (start us, length us, event | category | flops | bytes accessed | tf_op | source)
XLA Modules:
  0.0 96.0 jit_solution(7002982383411512159)
XLA Ops:
  0.6 0.0 copy-start
  0.6 90.2 %shard_map.77 = (f32[8,128,256]{2,1,0:T(8,128)}, f32[512,256]{1,0:T(8,128)}) custom-call(s32[32,32]{1,0:T(8,128)} %pick.1, f32[8,128,256]{2,1,0:T(8,128)} %bitcast.11, f32[512,256]{1,0:T(8,128)} %user_wide.1, bf16[8,4,512,128]{3,2,1,0:T(8,128)(2,1)} %bitcast.10), custom_call_target="tpu_custom_call" | custom-call | tf_op jit(solution)/shard_map/pallas_call | solution.py:431
  90.9 0.0 copy-done
  90.9 2.1 %multiply_add_fusion = f32[512,256]{1,0:T(8,128)} fusion(f32[512,256]{1,0:T(8,128)} %param.10, f32[512,256]{1,0:T(8,128)S(1)} %copy-done, f32[512,256]{1,0:T(8,128)} %get-tuple-element.4), kind=kLoop, calls=%fused_computation.4 | loop fusion | flops 655360 | bytes 2097152 | tf_op jit(solution)/shard_map/add | solution.py:471
  93.0 3.0 %fusion.2 = f32[1024,256]{1,0:T(8,128)} fusion(f32[1024,256]{1,0:T(8,128)} %param.7, f32[8,128,256]{2,1,0:T(8,128)} %get-tuple-element.5, f32[1024,256]{1,0:T(8,128)} %param.11), kind=kLoop, calls=%fused_computation.3 | loop fusion | flops 1310720 | bytes 4194304 | tf_op jit(solution)/shard_map/add | solution.py:470
Async XLA Ops:
  0.6 90.3 %copy-start = (f32[512,256]{1,0:T(8,128)S(1)}, f32[512,256]{1,0:T(8,128)}, u32[]{:S(2)}) copy-start(f32[512,256]{1,0:T(8,128)} %user_wide.1) | copy-start | bytes 1572868

commit v3 on v2

--- a/solution.py
+++ b/solution.py
@@ -39,11 +39,11 @@
 
 
 def kernel(
-    U, Z, H, pick, items_wide, user_wide, feedback, item_out, user_out, *scratch
+    U, Z, H, pick, items_wide, user_wide, feedback, item_noise, user_noise, item_out, user_out, *scratch
 ):
     held = scratch[:H]
     zbufs = scratch[H: H + 2 * (Z - 1) * H]
-    (user, og, arr, gs, gr, cs, cr, crd, fb, us, ur, xr, ws, wr, ug, values, sums, zsend, zrecv, isend, irecv, gsend,
+    (item_rand, user_rand, nsem, user, og, arr, gs, gr, cs, cr, crd, fb, us, ur, xr, ws, wr, ug, values, sums, zsend, zrecv, isend, irecv, gsend,
      grecv, csend, crecv, cdrecv, fsem, usend, urecv, xrecv, wsend, wrecv) = scratch[H + 2 * (Z - 1) * H:]
     B, T, K = items_wide.shape
     R = T // H
@@ -261,6 +261,10 @@
         for h in range(H):
             spread(z, h, held[h])
     ug[...] = jnp.zeros_like(ug)
+    item_fetch = pltpu.make_async_copy(item_noise, item_rand, nsem.at[0])
+    user_fetch = pltpu.make_async_copy(user_noise, user_rand, nsem.at[1])
+    item_fetch.start()
+    user_fetch.start()
 
     with jax.named_scope("compute_own"):
         def own(h, c):
@@ -321,6 +325,11 @@
         pl.when(jnp.logical_not(middle))(lambda: in_copy(z + inward, q).start())
         return carry
 
+    def set_user(rows, grad):
+        held_user = user_wide[rows, :]
+        user_out[rows, :] = (
+            held_user - step_size * (grad + prior_weight * held_user) + noise_scale * user_rand[rows, :])
+
     def users_out(q, carry):
         rows = rows_q(q)
 
@@ -329,13 +338,13 @@
             cross_copy(z, q).wait_recv()
             encode(ws.at[q], decode(us.at[q], user_unit) + decode(xr.at[q], user_unit), user_unit)
             pl.when(jnp.logical_not(edge))(lambda: out_copy(ws, z - inward, q).start())
-            user_out[rows, :] = decode(ws.at[q], user_unit)
+            set_user(rows, decode(ws.at[q], user_unit))
 
         @pl.when(jnp.logical_not(middle))
         def _():
             out_copy(ws, z, q).wait_recv()
             pl.when(jnp.logical_not(edge))(lambda: out_copy(wr, z - inward, q).start())
-            user_out[rows, :] = decode(wr.at[q], user_unit)
+            set_user(rows, decode(wr.at[q], user_unit))
         return carry
 
     def users_back():
@@ -347,6 +356,7 @@
             return c
         lax.fori_loop(first, last, one, 0)
 
+    user_fetch.wait()
     with jax.named_scope("users_in"):
         lax.fori_loop(0, PIECES, users_in, 0)
     with jax.named_scope("phase_a"):
@@ -379,11 +389,16 @@
             def _():
                 pl.when(lax.rem(b, RUN) == 0)(lambda: last_copy(z, z, h, c).wait_recv())
                 item_out[b, rows, :] += decode(crd.at[h, c], item_unit, at, R)
+            held_item = items_wide[b, rows, :]
+            item_out[b, rows, :] = (
+                held_item - item_step * (item_out[b, rows, :] + prior_weight * held_item)
+                + item_noise_scale * item_rand[b, rows, :])
             return carry
 
         lax.fori_loop(0, B, one, 0)
         return carry
 
+    item_fetch.wait()
     with jax.named_scope("finish"):
         lax.fori_loop(0, H, finish, 0)
 
@@ -416,7 +431,7 @@
         pl.when(jnp.logical_not(edge))(lambda q=q: out_copy(ws, z - inward, q).wait_send())
 
 
-def exchange(pick, items, user, feedback, U, Z):
+def exchange(pick, items, user, feedback, item_noise, user_noise, U, Z):
     B, T, K = items.shape
     N = user.shape[0]
     H = HALVES
@@ -431,9 +446,12 @@
     return pl.pallas_call(
         functools.partial(kernel, U, Z, H),
         out_shape=(jax.ShapeDtypeStruct((B, T, K), jnp.float32), jax.ShapeDtypeStruct((N, K), jnp.float32)),
-        in_specs=[pl.BlockSpec(memory_space=pltpu.SMEM), vmem, vmem, pl.BlockSpec(memory_space=pl.ANY)],
+        in_specs=[pl.BlockSpec(memory_space=pltpu.SMEM), vmem, vmem] + [pl.BlockSpec(memory_space=pl.ANY)] * 3,
         out_specs=(vmem, vmem),
         scratch_shapes=[pltpu.VMEM((B, R, K), bf16)] * (H * (2 * (Z - 1) + 1)) + [
+            pltpu.VMEM((B, T, K), jnp.float32),
+            pltpu.VMEM((N, K), jnp.float32),
+            dma((2,)),
             pltpu.VMEM((N, K), bf16),
             pltpu.VMEM((Z, H, U, R, K), bf16),
             pltpu.VMEM((Z, H, U, R, K), bf16),
@@ -455,7 +473,7 @@
         ],
         compiler_params=pltpu.CompilerParams(
             collective_id=0, has_side_effects=True, vmem_limit_bytes=63 * 2**20),
-    )(pick, items, user, feedback)
+    )(pick, items, user, feedback, item_noise, user_noise)
 
 
 def local(user_factors, item_factors, feedback, item_pick, user_noise, item_noise):
@@ -463,13 +481,10 @@
     tile, rank = feedback.shape[2], item_factors.shape[1]
     held = item_factors.shape[0] // tile
     items = item_factors.reshape(held, tile, rank)
-    item_grad, user_grad = exchange(
-        item_pick, items, user_factors,
-        feedback.reshape(U, Z, feedback.shape[1], tile), U, Z)
-    item_grad = item_grad.reshape(item_factors.shape)
-    new_item = item_factors - item_step * (item_grad + prior_weight * item_factors) + item_noise_scale * item_noise
-    new_user = user_factors - step_size * (user_grad + prior_weight * user_factors) + noise_scale * user_noise
-    return (new_user, new_item)
+    new_item, new_user = exchange(
+        item_pick, items, user_factors, feedback.reshape(U, Z, feedback.shape[1], tile),
+        item_noise.reshape(items.shape), user_noise, U, Z)
+    return (new_user, new_item.reshape(item_factors.shape))
 
 
 def solution(mesh):

time: 96.3 us -> 95.4 us (level)
  other arithmetic: 5.13 us -> 0 us
  local copies, waits for them, and re-layouts: 0.01 us -> 4.13 us
    add x2 -> x0, other arithmetic: 5.13 us -> none  [the longest x1 3.03 us: local(): item_factors - item_step * (item_grad + prior_weight * item_factors)]
    unnamed x2, local copies, waits for them, and re-layouts: 0.01 us -> 4.13 us
where the time goes in v3:
time: 95.4 us; the launch traced here: 95.1 us
  Pallas kernels  90.3 us (95%)
  local copies, waits for them, and re-layouts  4.13 us (4%)
    pallas_call x1, Pallas kernels, exchange(): pl.pallas_call(functools.partial(kernel, U, Z, H), out_shape=(jax.ShapeDt...  90.3 us
    unnamed x2, local copies, waits for them, and re-layouts  4.13 us

profile of v3, /device:TPU:0, one launch (start us, length us, event | category | flops | bytes accessed | tf_op | source)
XLA Modules:
  0.0 95.1 jit_solution(11104659227851518244)
XLA Ops:
  0.6 90.3 %shard_map.77 = (f32[8,128,256]{2,1,0:T(8,128)}, f32[512,256]{1,0:T(8,128)}) custom-call(s32[32,32]{1,0:T(8,128)} %pick.1, f32[8,128,256]{2,1,0:T(8,128)} %bitcast.5, f32[512,256]{1,0:T(8,128)} %user_wide.1, bf16[8,4,512,128]{3,2,1,0:T(8,128)(2,1)} %bitcast.4, f32[8,128,256]{2,1,0:T(8,128)} %bitcast.6, f32[512,256]{1,0:T(8,128)} %user_noise.1), custom_call_target="tpu_custom_call" | custom-call | tf_op jit(solution)/shard_map/pallas_call | solution.py:446
  91.0 1.9 %copy.10 = f32[512,256]{1,0:T(8,128)} copy(f32[512,256]{1,0:T(8,128)} %get-tuple-element.8) | data formatting | bytes 1048576
  92.9 2.3 %copy.11 = f32[1024,256]{1,0:T(8,128)} copy(f32[1024,256]{1,0:T(8,128)} %bitcast.7) | data formatting | bytes 2097152

commit v4 on v3

--- a/solution.py
+++ b/solution.py
@@ -39,13 +39,13 @@
 
 
 def kernel(
-    U, Z, H, pick, items_wide, user_wide, feedback, item_noise, user_noise, item_out, user_out, *scratch
+    U, Z, H, pick, items_far, user_far, feedback, item_noise, user_noise, item_home, user_home, *scratch
 ):
     held = scratch[:H]
     zbufs = scratch[H: H + 2 * (Z - 1) * H]
-    (item_rand, user_rand, nsem, user, og, arr, gs, gr, cs, cr, crd, fb, us, ur, xr, ws, wr, ug, values, sums, zsend, zrecv, isend, irecv, gsend,
+    (item_out, user_out, osem, psem, items_wide, user_wide, item_rand, user_rand, nsem, user, og, arr, gs, gr, cs, cr, crd, fb, us, ur, xr, ws, wr, ug, values, sums, zsend, zrecv, isend, irecv, gsend,
      grecv, csend, crecv, cdrecv, fsem, usend, urecv, xrecv, wsend, wrecv) = scratch[H + 2 * (Z - 1) * H:]
-    B, T, K = items_wide.shape
+    B, T, K = items_far.shape
     R = T // H
     N = user.shape[0]
     G = fb.shape[1]
@@ -63,6 +63,10 @@
             device_id={axis: to}, device_id_type=pl.DeviceIdType.MESH)
 
     barrier = pltpu.get_barrier_semaphore()
+    items_fetch = pltpu.make_async_copy(items_far, items_wide, nsem.at[2])
+    users_fetch = pltpu.make_async_copy(user_far, user_wide, nsem.at[3])
+    items_fetch.start()
+    users_fetch.start()
 
     def greet_user(j, c):
         pl.semaphore_signal(barrier, inc=1, device_id={"user": lax.rem(me + j, U)}, device_id_type=pl.DeviceIdType.MESH)
@@ -75,6 +79,7 @@
     def rows_of(h):
         return pl.ds(pl.multiple_of(lax.rem(me + h, H) * R, R), R)
 
+    items_fetch.wait()
     for h in range(H):
         held[h][...] = items_wide[:, rows_of(h), :].astype(jnp.bfloat16)
 
@@ -97,6 +102,7 @@
         for way in (0, 1):
             pl.when(can_send(1, way))(lambda way=way, h=h: zcopy(1, way, h).start())
 
+    users_fetch.wait()
     user[...] = user_wide[...].astype(jnp.bfloat16)
 
     def slot_of(o, h):
@@ -191,34 +197,32 @@
     def last_copy(to, p, h, c):
         return far("item", to, cs.at[p, h, c], crd.at[h, c], csend.at[p, h, c], cdrecv.at[h, c])
 
-    def phase(r, h, begin, end):
-        def target(way):
-            return r + way * (Z - 1 - 2 * r)
-
-        def active(way):
-            return (way == 0) & (z < r) | (way == 1) & (z > Z - 1 - r)
-
-        def source(way):
-            return (way == 0) & (z == 0) | (way == 1) & (z == Z - 1)
-
-        def in_turn(k):
-            return lax.rem(k + jnp.where(2 * z < Z - 1, 0, 1), 2)
-
-        def gather(k, carry):
-            way = in_turn(k)
-            pl.when(active(way))(lambda: collect(target(way), h, way))
-            return carry
-        lax.fori_loop(begin, end, gather, 0)
-
-        def pass_on(c, way):
-            p = target(way)
+    def target(r, way):
+        return r + way * (Z - 1 - 2 * r)
+
+    def active(r, way):
+        return (way == 0) & (z < r) | (way == 1) & (z > Z - 1 - r)
+
+    def in_turn(k):
+        return lax.rem(k + jnp.where(2 * z < Z - 1, 0, 1), 2)
+
+    def gather(r, h, k, bank):
+        way = in_turn(k)
+        pl.when(active(r, way))(lambda: collect(target(r, way), h, 2 * bank + way))
+
+    def pass_on(r, h, k, c, bank):
+        way = in_turn(k)
+
+        @pl.when(active(r, way))
+        def _():
+            p = target(r, way)
             to = z + 1 - 2 * way
-            relay = jnp.logical_not(source(way))
+            relay = (way == 0) & (z > 0) | (way == 1) & (z < Z - 1)
             pl.when(relay)(lambda: up_copy(z, p, h, c).wait_recv())
 
             def one(i, carry):
                 at = pl.ds(pl.multiple_of(i * R, R), R)
-                sums[at, :] = dense(p, c * RUN + i, way)
+                sums[at, :] = dense(p, c * RUN + i, 2 * bank + way)
 
                 @pl.when(relay)
                 def _():
@@ -230,11 +234,14 @@
             pl.when(last)(lambda: last_copy(to, p, h, c).start())
             pl.when(jnp.logical_not(last))(lambda: up_copy(to, p, h, c).start())
 
-        def one(k, carry):
-            way = in_turn(k // runs)
-            pl.when(active(way))(lambda: pass_on(lax.rem(k, runs), way))
+    def phase(r, h):
+        for k in range(2):
+            gather(r, h, k, 0)
+
+        def one(i, carry):
+            pass_on(r, h, i // runs, lax.rem(i, runs), 0)
             return carry
-        lax.fori_loop(begin * runs, end * runs, one, 0)
+        lax.fori_loop(0, 2 * runs, one, 0)
 
     def plane(d, way):
         return z - d if way == 0 else z + d
@@ -292,7 +299,7 @@
             pl.when(jnp.logical_not(edge) & (d == farthest) & (h == H - 1))(own_out)
         with jax.named_scope("phase"):
             ready = s - jnp.where(edge, 1, 0)
-            pl.when((ready >= 0) & (ready < (Z - 2) * H))(lambda: phase(ready // H + 1, lax.rem(ready, H), 0, 2))
+            pl.when((ready >= 0) & (ready < (Z - 2) * H))(lambda: phase(ready // H + 1, lax.rem(ready, H)))
         return carry
 
     lax.fori_loop(0, steps, step, 0)
@@ -325,6 +332,13 @@
         pl.when(jnp.logical_not(middle))(lambda: in_copy(z + inward, q).start())
         return carry
 
+    def user_back(q):
+        return pltpu.make_async_copy(user_out.at[rows_q(q)], user_home.at[rows_q(q)], psem.at[q])
+
+    def item_back(h, c):
+        part = pl.ds(c * RUN, RUN)
+        return pltpu.make_async_copy(item_out.at[part, rows_of(h)], item_home.at[part, rows_of(h)], osem.at[h, c])
+
     def set_user(rows, grad):
         held_user = user_wide[rows, :]
         user_out[rows, :] = (
@@ -339,13 +353,52 @@
             encode(ws.at[q], decode(us.at[q], user_unit) + decode(xr.at[q], user_unit), user_unit)
             pl.when(jnp.logical_not(edge))(lambda: out_copy(ws, z - inward, q).start())
             set_user(rows, decode(ws.at[q], user_unit))
+            user_back(q).start()
 
         @pl.when(jnp.logical_not(middle))
         def _():
             out_copy(ws, z, q).wait_recv()
             pl.when(jnp.logical_not(edge))(lambda: out_copy(wr, z - inward, q).start())
             set_user(rows, decode(wr.at[q], user_unit))
+            user_back(q).start()
         return carry
+
+    def drain_ingest():
+        for d in range(1, Z):
+            for way in (0, 1):
+                for h in range(H):
+                    pl.when(can_send(d, way))(lambda d=d, way=way, h=h: zcopy(d, way, h).wait_send())
+
+        def drain(j, c):
+            to = lax.rem(me + j, U)
+
+            def one(k, c):
+                icopy(k // H, lax.rem(k, H), to, me).wait_send()
+                gcopy(k // H, lax.rem(k, H), to, me).wait_send()
+                return c
+            return lax.fori_loop(0, Z * H, one, c)
+
+        lax.fori_loop(1, U, drain, 0)
+
+    def users_back():
+        lax.fori_loop(0, PIECES, users_out, 0)
+
+    def drain_ingest():
+        for d in range(1, Z):
+            for way in (0, 1):
+                for h in range(H):
+                    pl.when(can_send(d, way))(lambda d=d, way=way, h=h: zcopy(d, way, h).wait_send())
+
+        def drain(j, c):
+            to = lax.rem(me + j, U)
+
+            def one(k, c):
+                icopy(k // H, lax.rem(k, H), to, me).wait_send()
+                gcopy(k // H, lax.rem(k, H), to, me).wait_send()
+                return c
+            return lax.fori_loop(0, Z * H, one, c)
+
+        lax.fori_loop(1, U, drain, 0)
 
     def users_back():
         lax.fori_loop(0, PIECES, users_out, 0)
@@ -357,19 +410,29 @@
         lax.fori_loop(first, last, one, 0)
 
     user_fetch.wait()
+    pl.when(jnp.logical_not(edge))(drain_ingest)
     with jax.named_scope("users_in"):
         lax.fori_loop(0, PIECES, users_in, 0)
-    with jax.named_scope("phase_a"):
-        last_phase(0, H - 1, 0)
-    with jax.named_scope("users_mid"):
-        pl.when(middle)(users_back)
-    with jax.named_scope("phase_b"):
-        last_phase(0, H - 1, 1)
-    with jax.named_scope("phase_c"):
-        last_phase(H - 1, H, 0)
-    pl.when(edge)(own_out)
-    with jax.named_scope("phase_d"):
-        last_phase(H - 1, H, 1)
+    def last_order(i, carry):
+        inside = (i >= runs) & (i < 3 * runs)
+        j = i - runs
+        h = jnp.where(inside, lax.rem(j, 2), i // (2 * runs))
+        k = jnp.where(inside, 1 - lax.rem(j, 2), i // (2 * runs))
+        c = jnp.where(inside, j // 2, lax.rem(i, runs))
+
+        @pl.when(i == runs)
+        def _():
+            pl.when(middle)(users_back)
+            gather(Z - 1, 0, 1, 0)
+            gather(Z - 1, H - 1, 0, 1)
+            gather(Z - 1, H - 1, 1, 1)
+        pl.when((i == 3 * runs) & edge)(own_out)
+        pass_on(Z - 1, h, k, c, h)
+        return carry
+
+    gather(Z - 1, 0, 0, 0)
+    lax.fori_loop(0, 4 * runs, last_order, 0)
+    pl.when(edge)(drain_ingest)
 
     def finish(h, carry):
         collect(z, h, 0)
@@ -393,6 +456,7 @@
             item_out[b, rows, :] = (
                 held_item - item_step * (item_out[b, rows, :] + prior_weight * held_item)
                 + item_noise_scale * item_rand[b, rows, :])
+            pl.when(lax.rem(b, RUN) == RUN - 1)(lambda: item_back(h, c).start())
             return carry
 
         lax.fori_loop(0, B, one, 0)
@@ -405,27 +469,17 @@
     with jax.named_scope("userout"):
         pl.when(jnp.logical_not(middle))(users_back)
 
-    for d in range(1, Z):
-        for way in (0, 1):
-            for h in range(H):
-                pl.when(can_send(d, way))(lambda d=d, way=way, h=h: zcopy(d, way, h).wait_send())
-
-    def drain(j, c):
-        to = lax.rem(me + j, U)
-
-        def one(k, c):
-            icopy(k // H, lax.rem(k, H), to, me).wait_send()
-            gcopy(k // H, lax.rem(k, H), to, me).wait_send()
-            return c
-        return lax.fori_loop(0, Z * H, one, c)
-
-    lax.fori_loop(1, U, drain, 0)
     for j in range(1, Z):
         to = lax.rem(z + j, Z)
         def drained(k, c):
             up_copy(z, to, k // runs, lax.rem(k, runs)).wait_send()
             return c
         lax.fori_loop(0, H * runs, drained, 0)
+    for q in range(PIECES):
+        user_back(q).wait()
+    for h in range(H):
+        for c in range(runs):
+            item_back(h, c).wait()
     for q in range(PIECES):
         in_copy(z + inward, q).wait_send()
         pl.when(jnp.logical_not(edge))(lambda q=q: out_copy(ws, z - inward, q).wait_send())
@@ -442,16 +496,21 @@
     dma = pltpu.SemaphoreType.DMA
     i16 = jnp.int16
     bf16 = jnp.bfloat16
-    vmem = pl.BlockSpec(memory_space=pltpu.VMEM)
     return pl.pallas_call(
         functools.partial(kernel, U, Z, H),
         out_shape=(jax.ShapeDtypeStruct((B, T, K), jnp.float32), jax.ShapeDtypeStruct((N, K), jnp.float32)),
-        in_specs=[pl.BlockSpec(memory_space=pltpu.SMEM), vmem, vmem] + [pl.BlockSpec(memory_space=pl.ANY)] * 3,
-        out_specs=(vmem, vmem),
+        in_specs=[pl.BlockSpec(memory_space=pltpu.SMEM), ] + [pl.BlockSpec(memory_space=pl.ANY)] * 5,
+        out_specs=(pl.BlockSpec(memory_space=pl.ANY),) * 2,
         scratch_shapes=[pltpu.VMEM((B, R, K), bf16)] * (H * (2 * (Z - 1) + 1)) + [
             pltpu.VMEM((B, T, K), jnp.float32),
             pltpu.VMEM((N, K), jnp.float32),
-            dma((2,)),
+            dma((H, runs)),
+            dma((PIECES,)),
+            pltpu.VMEM((B, T, K), jnp.float32),
+            pltpu.VMEM((N, K), jnp.float32),
+            pltpu.VMEM((B, T, K), jnp.float32),
+            pltpu.VMEM((N, K), jnp.float32),
+            dma((4,)),
             pltpu.VMEM((N, K), bf16),
             pltpu.VMEM((Z, H, U, R, K), bf16),
             pltpu.VMEM((Z, H, U, R, K), bf16),
@@ -463,7 +522,7 @@
             pltpu.VMEM((4, G, N, T), bf16),
         ] + [pltpu.VMEM((PIECES, piece + PAD, K), i16)] * 5 + [
             pltpu.VMEM((N, K), jnp.float32),
-            pltpu.VMEM((2, U, R, K), jnp.float32),
+            pltpu.VMEM((2 * H, U, R, K), jnp.float32),
             pltpu.VMEM((RUN * R, K), jnp.float32),
             dma((2 * (Z - 1) * H,)), dma((2 * (Z - 1) * H,)),
             dma((Z, H, U)), dma((Z, H, U)), dma((Z, H, U)), dma((Z, H, U)),

time: 95.4 us -> 94.2 us (0.987)
  Pallas kernels: 90.3 us -> 89.1 us
    pallas_call x1, Pallas kernels: 90.3 us -> 89.1 us  [exchange(): pl.pallas_call(functools.partial(kernel, U, Z, H), out_shape=(jax.ShapeDt...]
where the time goes in v4:
time: 94.2 us; the launch traced here: 93.9 us
  Pallas kernels  89.1 us (95%)
  local copies, waits for them, and re-layouts  4.13 us (4%)
    pallas_call x1, Pallas kernels, exchange(): pl.pallas_call(functools.partial(kernel, U, Z, H), out_shape=(jax.ShapeDt...  89.1 us
    unnamed x2, local copies, waits for them, and re-layouts  4.13 us

profile of v4, /device:TPU:0, one launch (start us, length us, event | category | flops | bytes accessed | tf_op | source)
XLA Modules:
  0.0 93.9 jit_solution(13935501914509073103)
XLA Ops:
  0.6 89.1 %shard_map.77 = (f32[8,128,256]{2,1,0:T(8,128)}, f32[512,256]{1,0:T(8,128)}) custom-call(s32[32,32]{1,0:T(8,128)} %pick.1, f32[8,128,256]{2,1,0:T(8,128)} %bitcast.5, f32[512,256]{1,0:T(8,128)} %user_far.1, bf16[8,4,512,128]{3,2,1,0:T(8,128)(2,1)} %bitcast.4, f32[8,128,256]{2,1,0:T(8,128)} %bitcast.6, f32[512,256]{1,0:T(8,128)} %user_noise.1), custom_call_target="tpu_custom_call" | custom-call | tf_op jit(solution)/shard_map/pallas_call | solution.py:499
  89.8 1.9 %copy.10 = f32[512,256]{1,0:T(8,128)} copy(f32[512,256]{1,0:T(8,128)} %get-tuple-element.8) | data formatting | bytes 1048576
  91.6 2.3 %copy.11 = f32[1024,256]{1,0:T(8,128)} copy(f32[1024,256]{1,0:T(8,128)} %bitcast.7) | data formatting | bytes 2097152

commit v5 on v4

--- a/solution.py
+++ b/solution.py
@@ -20,6 +20,7 @@
 RUN = 4
 PAD = 8
 PIECES = 4
+CUTS = 4
 
 
 def encode(ref, value, unit):
@@ -535,6 +536,37 @@
     )(pick, items, user, feedback, item_noise, user_noise)
 
 
+def settle(items_in, users_in, items_out, users_out, items_held, users_held, insem, outsem):
+    parts = []
+    for src, held, dst in ((items_in, items_held, items_out), (users_in, users_held, users_out)):
+        rows = src.shape[0] // CUTS
+        parts += [(src.at[pl.ds(i * rows, rows)], held.at[pl.ds(i * rows, rows)], dst.at[pl.ds(i * rows, rows)])
+                  for i in range(CUTS)]
+    first = [pltpu.make_async_copy(src, held, insem.at[i]) for i, (src, held, _) in enumerate(parts)]
+    second = [pltpu.make_async_copy(held, dst, outsem.at[i]) for i, (_, held, dst) in enumerate(parts)]
+    for copy in first:
+        copy.start()
+    for copy, onward in zip(first, second):
+        copy.wait()
+        onward.start()
+    for onward in second:
+        onward.wait()
+
+
+def keep(items, users):
+    anywhere = pl.BlockSpec(memory_space=pl.ANY)
+    return pl.pallas_call(
+        settle,
+        out_shape=(jax.ShapeDtypeStruct(items.shape, items.dtype), jax.ShapeDtypeStruct(users.shape, users.dtype)),
+        in_specs=[anywhere] * 2,
+        out_specs=(anywhere,) * 2,
+        scratch_shapes=[
+            pltpu.VMEM(items.shape, items.dtype), pltpu.VMEM(users.shape, users.dtype),
+            pltpu.SemaphoreType.DMA((2 * CUTS,)), pltpu.SemaphoreType.DMA((2 * CUTS,)),
+        ],
+    )(items, users)
+
+
 def local(user_factors, item_factors, feedback, item_pick, user_noise, item_noise):
     U, Z = lax.axis_size("user"), lax.axis_size("item")
     tile, rank = feedback.shape[2], item_factors.shape[1]
@@ -543,7 +575,8 @@
     new_item, new_user = exchange(
         item_pick, items, user_factors, feedback.reshape(U, Z, feedback.shape[1], tile),
         item_noise.reshape(items.shape), user_noise, U, Z)
-    return (new_user, new_item.reshape(item_factors.shape))
+    new_item, new_user = keep(new_item.reshape(item_factors.shape), new_user)
+    return (new_user, new_item)
 
 
 def solution(mesh):

time: 94.2 us -> 92.3 us (0.980)
  local copies, waits for them, and re-layouts: 4.13 us -> 0 us
  Pallas kernels: 89.1 us -> 91.3 us
    unnamed x2 -> x0, local copies, waits for them, and re-layouts: 4.13 us -> none
    pallas_call x0 -> x1, Pallas kernels: none -> 2.22 us  [keep(): pl.pallas_call(settle, out_shape=(jax.ShapeDtypeStruct(items.shape, items...]
where the time goes in v5:
time: 92.3 us; the launch traced here: 92 us
  Pallas kernels  91.3 us (99%)
    pallas_call x1, Pallas kernels, exchange(): pl.pallas_call(functools.partial(kernel, U, Z, H), out_shape=(jax.ShapeDt...  89.1 us
    pallas_call x1, Pallas kernels, keep(): pl.pallas_call(settle, out_shape=(jax.ShapeDtypeStruct(items.shape, items...  2.22 us

profile of v5, /device:TPU:0, one launch (start us, length us, event | category | flops | bytes accessed | tf_op | source)
XLA Modules:
  0.0 92.0 jit_solution(4665369757265782817)
XLA Ops:
  0.6 89.1 %shard_map.77 = (f32[8,128,256]{2,1,0:T(8,128)}, f32[512,256]{1,0:T(8,128)}) custom-call(s32[32,32]{1,0:T(8,128)} %pick.1, f32[8,128,256]{2,1,0:T(8,128)} %bitcast.5, f32[512,256]{1,0:T(8,128)} %user_far.1, bf16[8,4,512,128]{3,2,1,0:T(8,128)(2,1)} %bitcast.4, f32[8,128,256]{2,1,0:T(8,128)} %bitcast.6, f32[512,256]{1,0:T(8,128)} %user_noise.1), custom_call_target="tpu_custom_call" | custom-call | tf_op jit(solution)/shard_map/pallas_call | solution.py:500
  89.8 2.2 %shard_map.78 = (f32[1024,256]{1,0:T(8,128)}, f32[512,256]{1,0:T(8,128)}) custom-call(f32[1024,256]{1,0:T(8,128)} %bitcast.7, f32[512,256]{1,0:T(8,128)} %get-tuple-element.7.users_in), custom_call_target="tpu_custom_call" | custom-call | tf_op jit(solution)/shard_map/pallas_call | solution.py:558

commit v6 on v5

--- a/solution.py
+++ b/solution.py
@@ -113,7 +113,7 @@
         return j // H * H + lax.rem(j + H - h, H)
 
     def icopy(p, h, to, src):
-        return far("user", to, og.at[p, h, to], arr.at[p, h, slot_of(src, h)], isend.at[p, h, to], irecv.at[p, h, src])
+        return far("user", to, og.at[p, h, to], arr.at[p, h, slot_of(src, h)], isend, irecv.at[p, h, src])
 
     def spread(p, h, blocks):
         def one(j, c):
@@ -125,7 +125,7 @@
         arr[p, h, slot_of(me, h)] = blocks[pick[me * Z + z, me * Z + p]]
 
     def gcopy(p, h, to, src):
-        return far("user", to, gs.at[p, h, to], gr.at[p, h, src], gsend.at[p, h, to], grecv.at[p, h, src])
+        return far("user", to, gs.at[p, h, to], gr.at[p, h, src], gsend, grecv.at[p, h, src])
 
     def fcopy(p, g, at):
         return pltpu.make_async_copy(feedback.at[pl.ds(G * g, G), p], fb.at[at], fsem.at[at])
@@ -370,16 +370,9 @@
                 for h in range(H):
                     pl.when(can_send(d, way))(lambda d=d, way=way, h=h: zcopy(d, way, h).wait_send())
 
-        def drain(j, c):
-            to = lax.rem(me + j, U)
-
-            def one(k, c):
-                icopy(k // H, lax.rem(k, H), to, me).wait_send()
-                gcopy(k // H, lax.rem(k, H), to, me).wait_send()
-                return c
-            return lax.fori_loop(0, Z * H, one, c)
-
-        lax.fori_loop(1, U, drain, 0)
+        others = pl.ds(0, U - 1)
+        pltpu.make_async_copy(og.at[:, :, others], og.at[:, :, others], isend).wait()
+        pltpu.make_async_copy(gs.at[:, :, others], gs.at[:, :, others], gsend).wait()
 
     def users_back():
         lax.fori_loop(0, PIECES, users_out, 0)
@@ -390,16 +383,9 @@
                 for h in range(H):
                     pl.when(can_send(d, way))(lambda d=d, way=way, h=h: zcopy(d, way, h).wait_send())
 
-        def drain(j, c):
-            to = lax.rem(me + j, U)
-
-            def one(k, c):
-                icopy(k // H, lax.rem(k, H), to, me).wait_send()
-                gcopy(k // H, lax.rem(k, H), to, me).wait_send()
-                return c
-            return lax.fori_loop(0, Z * H, one, c)
-
-        lax.fori_loop(1, U, drain, 0)
+        others = pl.ds(0, U - 1)
+        pltpu.make_async_copy(og.at[:, :, others], og.at[:, :, others], isend).wait()
+        pltpu.make_async_copy(gs.at[:, :, others], gs.at[:, :, others], gsend).wait()
 
     def users_back():
         lax.fori_loop(0, PIECES, users_out, 0)
@@ -526,7 +512,7 @@
             pltpu.VMEM((2 * H, U, R, K), jnp.float32),
             pltpu.VMEM((RUN * R, K), jnp.float32),
             dma((2 * (Z - 1) * H,)), dma((2 * (Z - 1) * H,)),
-            dma((Z, H, U)), dma((Z, H, U)), dma((Z, H, U)), dma((Z, H, U)),
+            dma, dma((Z, H, U)), dma, dma((Z, H, U)),
             dma((Z, H, runs)), dma((Z, H, runs)), dma((H, runs)),
             dma((4,)),
             dma((PIECES,)), dma((PIECES,)), dma((PIECES,)), dma((PIECES,)), dma((PIECES,)),

time: 92.3 us -> 90.9 us (0.985)
  Pallas kernels: 91.3 us -> 90 us
    pallas_call x1, Pallas kernels: 89.1 us -> 87.7 us  [exchange(): pl.pallas_call(functools.partial(kernel, U, Z, H), out_shape=(jax.ShapeDt...]
where the time goes in v6:
time: 90.9 us; the launch traced here: 90.6 us
  Pallas kernels  90 us (99%)
    pallas_call x1, Pallas kernels, exchange(): pl.pallas_call(functools.partial(kernel, U, Z, H), out_shape=(jax.ShapeDt...  87.7 us
    pallas_call x1, Pallas kernels, keep(): pl.pallas_call(settle, out_shape=(jax.ShapeDtypeStruct(items.shape, items...  2.22 us

profile of v6, /device:TPU:0, one launch (start us, length us, event | category | flops | bytes accessed | tf_op | source)
XLA Modules:
  0.0 90.6 jit_solution(11930504601056973212)
XLA Ops:
  0.6 87.7 %shard_map.77 = (f32[8,128,256]{2,1,0:T(8,128)}, f32[512,256]{1,0:T(8,128)}) custom-call(s32[32,32]{1,0:T(8,128)} %pick.1, f32[8,128,256]{2,1,0:T(8,128)} %bitcast.5, f32[512,256]{1,0:T(8,128)} %user_far.1, bf16[8,4,512,128]{3,2,1,0:T(8,128)(2,1)} %bitcast.4, f32[8,128,256]{2,1,0:T(8,128)} %bitcast.6, f32[512,256]{1,0:T(8,128)} %user_noise.1), custom_call_target="tpu_custom_call" | custom-call | tf_op jit(solution)/shard_map/pallas_call | solution.py:486
  88.4 2.2 %shard_map.78 = (f32[1024,256]{1,0:T(8,128)}, f32[512,256]{1,0:T(8,128)}) custom-call(f32[1024,256]{1,0:T(8,128)} %bitcast.7, f32[512,256]{1,0:T(8,128)} %get-tuple-element.7.users_in), custom_call_target="tpu_custom_call" | custom-call | tf_op jit(solution)/shard_map/pallas_call | solution.py:544
